TPU v7x, 512 devices: a whole 4x4x16 slice. The times are simulated.
512 devices in a mesh: off: 16 (over z_lo, y), img: 32 (over x, z_hi, core).
Axes of the slice: x: 4, y: 4, z: 16 (z_hi: 4, z_lo: 4; z = z_hi * 4 + z_lo), core: 2. Of those that a mesh axis runs over, the one named last changes fastest.
Arguments:
- traces: bfloat16 [16384, 3072], P(('off', 'img')), may hold values from -6 to 6
- offset_bins: int32 [16384], P(('off', 'img')), may hold values from 0 to 15, as said below
- class_slots: int32 [16384], P(('off', 'img')), may hold values from 0 to 1, as said below
- weights: bfloat16 [16, 16384, 1024], P('off', 'img'), may hold values from -0.1875 to 0.1875
- band_start: int32 [16, 128], P('off', 'img'), may hold values from 0 to 1536
- smoothing: int32 [16, 128], P('off', 'img'), may hold values from 0 to 1
Outputs:
- migrated: bfloat16 [16, 16384, 1536], P('off', 'img')
Inputs may be any that keep to these rules, and one draw needn't show every extreme that they name: `offset_bins`: in each aligned block of 32 traces every class is named by exactly 2 traces. Within each aligned block of 32 traces the pairs (offset_bins, class_slots) are all distinct.
All inputs are finite; a program needn't handle non-finite values.
Results may differ from a plain program's by a relative error of at most 0.005.
Values may be sent and summed in bfloat16 or wider, within the bound.
No kernel may reach another device: no remote copies, remote signals or barrier semaphores. Data moves between devices by JAX's collectives and lax.ppermute only.
A program may use at most 128 MiB of HBM per device.

v0:
```python
import jax
import jax.numpy as jnp
from jax import lax
from jax.sharding import PartitionSpec as P

NT = 1536
CB = 128


def filtered_levels(samples):
    values = samples.astype(jnp.float32)
    edges = [(0, 0)] * (values.ndim - 1)
    padded = jnp.pad(values, edges + [(1, 1)])
    boosted = values - 0.5 * (padded[..., :-2] + padded[..., 2:])
    widened = jnp.pad(boosted, edges + [(2, 2)])
    smoothed = (
        3.0 * boosted
        + 2.0 * (widened[..., 1:-3] + widened[..., 3:-1])
        + widened[..., :-4]
        + widened[..., 4:]
    ) / 9.0
    return jnp.stack([boosted, smoothed]).astype(jnp.bfloat16)


def migrate_rows(summed, shard_rows, weight_rows, band_rows, smooth_rows):
    row_count = shard_rows.shape[1]

    def segment(level_index, offset):
        return lax.dynamic_slice(shard_rows, (level_index, 0, offset), (1, row_count, NT))[0]

    segments = jax.vmap(segment)(smooth_rows, band_rows)
    blocks = band_rows.shape[0]
    columns = weight_rows
    columns = columns.reshape(blocks, CB, row_count)
    update = jnp.einsum("bcr,brt->bct", columns, segments, preferred_element_type=jnp.float32)
    return update.reshape(summed.shape)


def per_device(traces, offset_bins, class_slots, weights, band_start, smoothing):
    tr_count = traces.shape[0]
    per_class = tr_count // lax.axis_size("off")
    targets = offset_bins * per_class + class_slots
    weight_rows = weights[0]
    band_rows = band_start[0]
    smooth_rows = smoothing[0]
    initial = jnp.zeros((weight_rows.shape[0], NT), jnp.float32)
    levels = filtered_levels(traces)
    ordered = jnp.zeros_like(levels).at[:, targets].set(levels)
    regrouped = lax.all_to_all(ordered, "off", split_axis=1, concat_axis=1, tiled=True)
    summed = migrate_rows(
        initial,
        lax.all_gather(regrouped, "img", axis=1, tiled=True),
        weight_rows,
        band_rows,
        smooth_rows,
    )
    return summed.astype(jnp.bfloat16)[None]


def solution(mesh):
    in_specs = (
        P(("off", "img"), None),
        P(("off", "img")),
        P(("off", "img")),
        P("off", "img", None),
        P("off", "img"),
        P("off", "img"),
    )
    out_specs = P("off", "img", None)
    return jax.shard_map(
        per_device, mesh=mesh, in_specs=in_specs, out_specs=out_specs, check_vma=False
    )
```

profile of v0, /device:TPU:5, one launch (start us, length us, event | category | flops | bytes accessed | tf_op | source)
XLA Modules:
  0.0 268.0 jit_solution(2371842476114070729)
XLA Ops:
  6.5 0.0 all-gather.2.cloned.1.call-start
  6.5 1.0 convert_element_type.24
  7.6 0.3 convert_bitcast_fusion
  7.9 0.5 fusion.8
  8.4 0.4 copy.10
  8.8 0.7 compare_select_fusion.2
  9.5 0.2 broadcast_in_dim.4
  9.7 1.5 scatter_fusion
  11.2 19.9 %all_to_all.5 = bf16[2,32,3072]{2,0,1:T(2,128)(2,1)} all-to-all(bf16[2,32,3072]{2,0,1:T(2,128)(2,1)S(1)} %scatter_fusion), channel_id=1, replica_groups=mesh['off'=16,'img'=32] {'off'}, dimensions={1} | all-to-all | bytes 786432 | tf_op jit(solution)/shard_map/all_to_all | solution.py:49
  31.2 0.0 all-gather.2.cloned.1.call-update
  31.2 0.7 compare_select_fusion
  31.9 0.1 copy.12
  32.0 180.9 %all-gather.2.cloned.1.call-done = bf16[2,1024,3072]{2,0,1:T(2,128)(2,1)} async-done(((bf16[2,32,3072]{2,0,1:T(2,128)(2,1)}), bf16[2,1024,3072]{2,0,1:T(2,128)(2,1)}) %all-gather.2.cloned.1.call-update) | async-done | bytes 12582928 | tf_op jit(solution)/shard_map/all_gather | solution.py:52
  212.9 12.6 %copy.11 = bf16[2,1024,3072]{2,1,0:T(8,128)(2,1)} copy(bf16[2,1024,3072]{2,0,1:T(2,128)(2,1)} %all-gather.2.cloned.1.call-done) | data formatting | bytes 25165824
  225.5 28.1 %while.1 = (s32[]{:T(128)}, bf16[2,1024,3072]{2,1,0:T(8,128)(2,1)}, s32[4,3]{1,0:T(4,128)S(1)}, bf16[4,1,1024,1536]{3,2,1,0:T(8,128)(2,1)}, s32[]{:T(128)}) while((s32[]{:T(128)}, bf16[2,1024,3072]{2,1,0:T(8,128)(2,1)}, s32[4,3]{1,0:T(4,128)S(1)}, bf16[4,1,1024,1536]{3,2,1,0:T(8,128)(2,1)}, s32[]{:T(128)}) %tuple.23), condition=%wide.while_cond, body=%wide.while_body.sunk | while | flops 2 | bytes 6293097 | solution.py:29
  225.5 0.6 fusion.13
  226.1 6.4 %bitcast_dynamic-update-slice_fusion.2 = bf16[4,1,1024,1536]{3,2,1,0:T(8,128)(2,1)} fusion(bf16[4,1,1024,1536]{3,2,1,0:T(8,128)(2,1)} %get-tuple-element.72, s32[]{:T(128)} %get-tuple-element.69, bf16[2,1024,3072]{2,1,0:T(8,128)(2,1)} %get-tuple-element.75, s32[]{:T(128)} %bitcast.28, s32[]{:T(128)} %bitcast.29), kind=kLoop, calls=%fused_computation.1.clone.1 | loop fusion | bytes 6292992 | tf_op jit(solution)/shard_map/vmap()/gather
  232.5 0.6 fusion.13
  233.2 6.4 %bitcast_dynamic-update-slice_fusion.2 = bf16[4,1,1024,1536]{3,2,1,0:T(8,128)(2,1)} fusion(bf16[4,1,1024,1536]{3,2,1,0:T(8,128)(2,1)} %get-tuple-element.72, s32[]{:T(128)} %get-tuple-element.69, bf16[2,1024,3072]{2,1,0:T(8,128)(2,1)} %get-tuple-element.75, s32[]{:T(128)} %bitcast.28, s32[]{:T(128)} %bitcast.29), kind=kLoop, calls=%fused_computation.1.clone.1 | loop fusion | bytes 6292992 | tf_op jit(solution)/shard_map/vmap()/gather
  239.6 0.6 fusion.13
  240.2 6.4 %bitcast_dynamic-update-slice_fusion.2 = bf16[4,1,1024,1536]{3,2,1,0:T(8,128)(2,1)} fusion(bf16[4,1,1024,1536]{3,2,1,0:T(8,128)(2,1)} %get-tuple-element.72, s32[]{:T(128)} %get-tuple-element.69, bf16[2,1024,3072]{2,1,0:T(8,128)(2,1)} %get-tuple-element.75, s32[]{:T(128)} %bitcast.28, s32[]{:T(128)} %bitcast.29), kind=kLoop, calls=%fused_computation.1.clone.1 | loop fusion | bytes 6292992 | tf_op jit(solution)/shard_map/vmap()/gather
  246.6 0.6 fusion.13
  247.2 6.4 %bitcast_dynamic-update-slice_fusion.2 = bf16[4,1,1024,1536]{3,2,1,0:T(8,128)(2,1)} fusion(bf16[4,1,1024,1536]{3,2,1,0:T(8,128)(2,1)} %get-tuple-element.72, s32[]{:T(128)} %get-tuple-element.69, bf16[2,1024,3072]{2,1,0:T(8,128)(2,1)} %get-tuple-element.75, s32[]{:T(128)} %bitcast.28, s32[]{:T(128)} %bitcast.29), kind=kLoop, calls=%fused_computation.1.clone.1 | loop fusion | bytes 6292992 | tf_op jit(solution)/shard_map/vmap()/gather
  253.6 7.5 %fusion.2 = bf16[4,1536,128]{1,2,0:T(8,128)(2,1)} fusion(bf16[4,128,1024]{2,1,0:T(8,128)(2,1)S(1)} %bitcast.30, bf16[4,1,1024,1536]{3,2,1,0:T(8,128)(2,1)} %get-tuple-element.12), kind=kOutput, calls=%fused_computation.5 | convolution fusion | flops 1611399168 | bytes 15204352 | tf_op jit(solution)/shard_map/bcr,brt->bct/dot_general | solution.py:35
  (10 shorter events, 0.1 us)
Async XLA Ops:
  6.5 247.1 %copy-start = (bf16[1,512,1024]{2,1,0:T(8,128)(2,1)S(1)}, bf16[1,512,1024]{2,1,0:T(8,128)(2,1)}, u32[]{:S(2)}) copy-start(bf16[1,512,1024]{2,1,0:T(8,128)(2,1)} %param.9) | copy-start | bytes 3145732
  6.5 206.3 %all-gather.2.cloned.1.call-start = ((), (), s32[]{:S(2)}) async-start(), calls=%async_computation.1 | async-start | bytes 12976128 | tf_op jit(solution)/shard_map/all_gather | solution.py:52
Sparse Core Ops, SparseCore 0:
  31.3 181.5 all-gather.1
where the time goes:
time: 268 us
  waiting for transfers between devices  181 us (68%)
  local copies, waits for them, and re-layouts  43 us (16%)
  blocking collectives  19.9 us (7%)
  between operations  13.4 us (5%)
  matrix products  7.54 us (3%)
  other arithmetic  3.2 us (1%)
    all_gather x1, waiting for transfers between devices, per_device(): lax.all_gather(regrouped, 'img', axis=1, tiled=True)  181 us
    gather x12, local copies, waits for them, and re-layouts  28.1 us
    all_to_all x1, blocking collectives, per_device(): lax.all_to_all(ordered, 'off', split_axis=1, concat_axis=1, tiled=True)  19.9 us
    unnamed x4, local copies, waits for them, and re-layouts  12.7 us
    dot_general x1, matrix products, migrate_rows(): jnp.einsum('bcr,brt->bct', columns, segments, preferred_element_type=jnp....  7.54 us
  transfers between devices with their start and end apart: 1, of which 1 were waited for; matrix products, arithmetic and copies ran while one was open for 0% of the time, Pallas kernels for 0%

commit v1 on v0

--- a/solution.py
+++ b/solution.py
@@ -46,7 +46,12 @@
     initial = jnp.zeros((weight_rows.shape[0], NT), jnp.float32)
     levels = filtered_levels(traces)
     ordered = jnp.zeros_like(levels).at[:, targets].set(levels)
-    regrouped = lax.all_to_all(ordered, "off", split_axis=1, concat_axis=1, tiled=True)
+    regrouped = jnp.concatenate(
+        jax.lax.all_to_all(
+            jnp.stack(jnp.split(ordered, jax.lax.axis_size("off"), axis=1)), "off", 0, 0
+        ),
+        axis=1,
+    )
     summed = migrate_rows(
         initial,
         lax.all_gather(regrouped, "img", axis=1, tiled=True),

time: 268 us -> 257 us (0.959)
  the two profiles are of different devices: /device:TPU:5 before, /device:TPU:3 now
where the time goes in v1:
time: 257 us
  waiting for transfers between devices  181 us (70%)
  local copies, waits for them, and re-layouts  31.5 us (12%)
  blocking collectives  19.8 us (8%)
  between operations  13.5 us (5%)
  matrix products  7.54 us (3%)
  other arithmetic  3.2 us (1%)
    all_gather x1, waiting for transfers between devices, per_device(): lax.all_gather(regrouped, 'img', axis=1, tiled=True)  181 us
    gather x12, local copies, waits for them, and re-layouts  28 us
    all_to_all x1, blocking collectives, per_device(): jax.lax.all_to_all(jnp.stack(jnp.split(ordered, jax.lax.axis_size('off'),...  19.8 us
    dot_general x1, matrix products, migrate_rows(): jnp.einsum('bcr,brt->bct', columns, segments, preferred_element_type=jnp....  7.54 us
  transfers between devices with their start and end apart: 1, of which 1 were waited for; matrix products, arithmetic and copies ran while one was open for 0% of the time, Pallas kernels for 0%

profile of v1, /device:TPU:3, one launch (start us, length us, event | category | flops | bytes accessed | tf_op | source)
XLA Modules:
  0.0 256.6 jit_solution(16643066821547088890)
XLA Ops:
  6.5 0.0 copy-start
  6.5 1.0 convert_element_type.24
  7.6 0.3 convert_bitcast_fusion
  7.9 0.5 fusion.8
  8.4 0.4 copy.7
  8.8 0.7 compare_select_fusion.2
  9.5 0.2 broadcast_in_dim.4
  9.7 1.5 scatter_fusion
  11.7 19.8 %all_to_all.5 = bf16[16,2,2,3072]{3,1,2,0:T(2,128)(2,1)S(1)} all-to-all(bf16[16,2,2,3072]{3,1,2,0:T(2,128)(2,1)S(1)} %constant_dynamic-update-slice_fusion), channel_id=1, replica_groups=mesh['off'=16,'img'=32] {'off'}, dimensions={0} | all-to-all | bytes 786432 | tf_op jit(solution)/shard_map/all_to_all | solution.py:50
  31.6 0.8 copy.8
  32.4 0.0 all-gather.2.cloned.1.call-update
  32.4 0.7 compare_select_fusion
  33.1 0.1 copy.9
  33.2 181.0 %all-gather.2.cloned.1.call-done = bf16[2,1024,3072]{2,1,0:T(8,128)(2,1)} async-done(((bf16[2,32,3072]{2,1,0:T(8,128)(2,1)}), bf16[2,1024,3072]{2,1,0:T(8,128)(2,1)}) %all-gather.2.cloned.1.call-update) | async-done | bytes 12582928 | tf_op jit(solution)/shard_map/all_gather | solution.py:57
  214.2 28.0 %while.1 = (s32[]{:T(128)}, bf16[2,1024,3072]{2,1,0:T(8,128)(2,1)}, s32[4,3]{1,0:T(4,128)S(1)}, bf16[4,1,1024,1536]{3,2,1,0:T(8,128)(2,1)}, s32[]{:T(128)}) while((s32[]{:T(128)}, bf16[2,1024,3072]{2,1,0:T(8,128)(2,1)}, s32[4,3]{1,0:T(4,128)S(1)}, bf16[4,1,1024,1536]{3,2,1,0:T(8,128)(2,1)}, s32[]{:T(128)}) %tuple.22), condition=%wide.while_cond, body=%wide.while_body.sunk | while | flops 2 | bytes 6293097 | solution.py:29
  214.2 0.6 fusion.13
  214.8 6.4 %bitcast_dynamic-update-slice_fusion.2 = bf16[4,1,1024,1536]{3,2,1,0:T(8,128)(2,1)} fusion(bf16[4,1,1024,1536]{3,2,1,0:T(8,128)(2,1)} %get-tuple-element.68, s32[]{:T(128)} %get-tuple-element.65, bf16[2,1024,3072]{2,1,0:T(8,128)(2,1)} %get-tuple-element.71, s32[]{:T(128)} %bitcast.95, s32[]{:T(128)} %bitcast.96), kind=kLoop, calls=%fused_computation.1.clone.1 | loop fusion | bytes 6292992 | tf_op jit(solution)/shard_map/vmap()/gather
  221.2 0.6 fusion.13
  221.8 6.4 %bitcast_dynamic-update-slice_fusion.2 = bf16[4,1,1024,1536]{3,2,1,0:T(8,128)(2,1)} fusion(bf16[4,1,1024,1536]{3,2,1,0:T(8,128)(2,1)} %get-tuple-element.68, s32[]{:T(128)} %get-tuple-element.65, bf16[2,1024,3072]{2,1,0:T(8,128)(2,1)} %get-tuple-element.71, s32[]{:T(128)} %bitcast.95, s32[]{:T(128)} %bitcast.96), kind=kLoop, calls=%fused_computation.1.clone.1 | loop fusion | bytes 6292992 | tf_op jit(solution)/shard_map/vmap()/gather
  228.2 0.6 fusion.13
  228.8 6.4 %bitcast_dynamic-update-slice_fusion.2 = bf16[4,1,1024,1536]{3,2,1,0:T(8,128)(2,1)} fusion(bf16[4,1,1024,1536]{3,2,1,0:T(8,128)(2,1)} %get-tuple-element.68, s32[]{:T(128)} %get-tuple-element.65, bf16[2,1024,3072]{2,1,0:T(8,128)(2,1)} %get-tuple-element.71, s32[]{:T(128)} %bitcast.95, s32[]{:T(128)} %bitcast.96), kind=kLoop, calls=%fused_computation.1.clone.1 | loop fusion | bytes 6292992 | tf_op jit(solution)/shard_map/vmap()/gather
  235.2 0.6 fusion.13
  235.8 6.4 %bitcast_dynamic-update-slice_fusion.2 = bf16[4,1,1024,1536]{3,2,1,0:T(8,128)(2,1)} fusion(bf16[4,1,1024,1536]{3,2,1,0:T(8,128)(2,1)} %get-tuple-element.68, s32[]{:T(128)} %get-tuple-element.65, bf16[2,1024,3072]{2,1,0:T(8,128)(2,1)} %get-tuple-element.71, s32[]{:T(128)} %bitcast.95, s32[]{:T(128)} %bitcast.96), kind=kLoop, calls=%fused_computation.1.clone.1 | loop fusion | bytes 6292992 | tf_op jit(solution)/shard_map/vmap()/gather
  242.2 7.5 %fusion.2 = bf16[4,1536,128]{1,2,0:T(8,128)(2,1)} fusion(bf16[4,128,1024]{2,1,0:T(8,128)(2,1)S(1)} %bitcast.97, bf16[4,1,1024,1536]{3,2,1,0:T(8,128)(2,1)} %get-tuple-element.12), kind=kOutput, calls=%fused_computation.5 | convolution fusion | flops 1611399168 | bytes 15204352 | tf_op jit(solution)/shard_map/bcr,brt->bct/dot_general | solution.py:35
  (26 shorter events, 0.5 us)
Async XLA Ops:
  6.5 235.7 %copy-start = (bf16[1,512,1024]{2,1,0:T(8,128)(2,1)S(1)}, bf16[1,512,1024]{2,1,0:T(8,128)(2,1)}, u32[]{:S(2)}) copy-start(bf16[1,512,1024]{2,1,0:T(8,128)(2,1)} %param.9) | copy-start | bytes 3145732
  6.5 207.7 %all-gather.2.cloned.1.call-start = ((), (), s32[]{:S(2)}) async-start(), calls=%async_computation.1 | async-start | bytes 12976128 | tf_op jit(solution)/shard_map/all_gather | solution.py:57
Sparse Core Ops, SparseCore 0:
  32.5 181.6 all-gather.1

commit v2 on v0

--- a/solution.py
+++ b/solution.py
@@ -5,6 +5,13 @@
 
 NT = 1536
 CB = 128
+
+
+def swapped_in(x, name, along):
+    size = lax.axis_size(name)
+    blocks = jnp.stack([x for _ in range(size)])
+    blocks = lax.all_to_all(blocks, name, split_axis=0, concat_axis=0)
+    return jnp.concatenate(blocks, axis=along)
 
 
 def filtered_levels(samples):
@@ -48,11 +55,7 @@
     ordered = jnp.zeros_like(levels).at[:, targets].set(levels)
     regrouped = lax.all_to_all(ordered, "off", split_axis=1, concat_axis=1, tiled=True)
     summed = migrate_rows(
-        initial,
-        lax.all_gather(regrouped, "img", axis=1, tiled=True),
-        weight_rows,
-        band_rows,
-        smooth_rows,
+        initial, swapped_in(regrouped, "img", 1), weight_rows, band_rows, smooth_rows
     )
     return summed.astype(jnp.bfloat16)[None]
 

time: 268 us -> 651 us (2.43)
  the two profiles are of different devices: /device:TPU:5 before, /device:TPU:474 now
where the time goes in v2:
time: 651 us; the launch traced here: 650 us
  waiting for transfers between devices  564 us (87%)
  local copies, waits for them, and re-layouts  47.7 us (7%)
  blocking collectives  15.5 us (2%)
  starting transfers between devices  13 us (2%)
  matrix products  7.54 us (1%)
    all_to_all x1, waiting for transfers between devices, swapped_in(): blocks = lax.all_to_all(blocks, name, split_axis=0, concat_axis=0)  564 us
    gather x12, local copies, waits for them, and re-layouts  28.3 us
    all_to_all x1, blocking collectives, per_device(): lax.all_to_all(ordered, 'off', split_axis=1, concat_axis=1, tiled=True)  15.5 us
  transfers between devices with their start and end apart: 1, of which 1 were waited for; matrix products, arithmetic and copies ran while one was open for 0% of the time, Pallas kernels for 0%

profile of v2, /device:TPU:474, one launch (start us, length us, event | category | flops | bytes accessed | tf_op | source)
XLA Modules:
  0.0 650.3 jit_solution(17077278491732739575)
XLA Ops:
  0.0 1.0 convert_element_type.24
  1.0 0.3 convert_bitcast_fusion
  1.3 0.5 fusion.8
  1.8 0.4 copy.13
  2.3 0.7 compare_select_fusion.2
  2.9 0.2 broadcast_in_dim.4
  3.2 1.5 scatter_fusion
  4.7 15.5 %all_to_all.10 = bf16[2,32,3072]{2,0,1:T(2,128)(2,1)S(1)} all-to-all(bf16[2,32,3072]{2,0,1:T(2,128)(2,1)S(1)} %scatter_fusion), channel_id=1, replica_groups=mesh['off'=16,'img'=32] {'off'}, dimensions={1} | all-to-all | bytes 786432 | tf_op jit(solution)/shard_map/all_to_all | solution.py:56
  20.2 0.1 copy.14
  20.3 6.1 stack.14
  26.4 13.0 %all-to-all-start.1 = ((bf16[32,2,32,3072]{3,2,1,0:T(8,128)(2,1)}), bf16[32,2,32,3072]{3,2,1,0:T(8,128)(2,1)}, u32[]{:S(2)}, u32[]{:S(2)}) async-start(bf16[32,2,32,3072]{3,2,1,0:T(8,128)(2,1)} %stack.14), calls=%async_computation.1 | async-start | bytes 25165824 | tf_op jit(solution)/shard_map/all_to_all | solution.py:13
  39.5 0.1 copy.16
  39.6 564.0 %all-to-all-done.1 = bf16[32,2,32,3072]{3,2,1,0:T(8,128)(2,1)} async-done(((bf16[32,2,32,3072]{3,2,1,0:T(8,128)(2,1)}), bf16[32,2,32,3072]{3,2,1,0:T(8,128)(2,1)}, u32[]{:S(2)}, u32[]{:S(2)}) %all-to-all-start.1) | async-done | bytes 12582944 | tf_op jit(solution)/shard_map/all_to_all | solution.py:13
  603.6 10.9 %copy.15 = bf16[32,2,32,3072]{3,2,0,1:T(8,128)(2,1)} copy(bf16[32,2,32,3072]{3,2,1,0:T(8,128)(2,1)} %all-to-all-done.1) | data formatting | bytes 25165824 | tf_op jit(solution)/shard_map/all_to_all | solution.py:13
  614.4 28.4 %while.1 = (s32[]{:T(128)}, bf16[2,1024,3072]{2,1,0:T(8,128)(2,1)}, s32[4,3]{1,0:T(4,128)S(1)}, bf16[4,1,1024,1536]{3,2,1,0:T(8,128)(2,1)}, s32[]{:T(128)}) while((s32[]{:T(128)}, bf16[2,1024,3072]{2,1,0:T(8,128)(2,1)}, s32[4,3]{1,0:T(4,128)S(1)}, bf16[4,1,1024,1536]{3,2,1,0:T(8,128)(2,1)}, s32[]{:T(128)}) %tuple.27), condition=%wide.while_cond, body=%wide.while_body.sunk | while | flops 2 | bytes 6293097 | solution.py:36
  614.5 0.6 fusion.13
  615.1 6.4 bitcast_dynamic-update-slice_fusion.2
  621.5 0.6 fusion.13
  622.2 6.4 bitcast_dynamic-update-slice_fusion.2
  628.6 0.6 fusion.13
  629.3 6.4 bitcast_dynamic-update-slice_fusion.2
  635.7 0.6 fusion.13
  636.3 6.5 bitcast_dynamic-update-slice_fusion.2
  642.8 7.5 %fusion.2 = bf16[4,1536,128]{1,2,0:T(8,128)(2,1)} fusion(bf16[4,128,1024]{2,1,0:T(8,128)(2,1)S(1)} %bitcast.33, bf16[4,1,1024,1536]{3,2,1,0:T(8,128)(2,1)} %get-tuple-element.12), kind=kOutput, calls=%fused_computation.5 | convolution fusion | flops 1611399168 | bytes 15204352 | tf_op jit(solution)/shard_map/bcr,brt->bct/dot_general | solution.py:42
  (15 shorter events, 0.1 us)
Async XLA Ops:
  0.0 642.8 %copy-start = (bf16[1,512,1024]{2,1,0:T(8,128)(2,1)S(1)}, bf16[1,512,1024]{2,1,0:T(8,128)(2,1)}, u32[]{:S(2)}) copy-start(bf16[1,512,1024]{2,1,0:T(8,128)(2,1)} %param.9) | copy-start | bytes 3145732
  26.4 13.0 %copy-start.1 = (s32[1,4]{1,0:T(1,128)S(1)}, s32[1,4]{1,0:T(1,128)}, u32[]{:S(2)}) copy-start(s32[1,4]{1,0:T(1,128)} %param.10) | copy-start | bytes 52
  26.4 13.0 %copy-start.2 = (s32[1,4]{1,0:T(1,128)S(1)}, s32[1,4]{1,0:T(1,128)}, u32[]{:S(2)}) copy-start(s32[1,4]{1,0:T(1,128)} %param.11) | copy-start | bytes 52
  26.4 577.1 %all-to-all-start.1 = ((bf16[32,2,32,3072]{3,2,1,0:T(8,128)(2,1)}), bf16[32,2,32,3072]{3,2,1,0:T(8,128)(2,1)}, u32[]{:S(2)}, u32[]{:S(2)}) async-start(bf16[32,2,32,3072]{3,2,1,0:T(8,128)(2,1)} %stack.14), calls=%async_computation.1 | async-start | bytes 25165824 | tf_op jit(solution)/shard_map/all_to_all | solution.py:13
